TPU v7x, 256 devices: a whole 4x4x8 slice. The times are simulated.
256 devices in a mesh: wide: 64 (over z, x, core), narrow: 4 (over y).
Axes of the slice: x: 4, y: 4, z: 8, core: 2. Of those that a mesh axis runs over, the one named last changes fastest.
Arguments:
- coeffs: bfloat16 [2, 1024, 1024, 512], P(None, 'wide', None, 'narrow'), may hold values from -3 to 3
- legendre: bfloat16 [1024, 64, 1024], P('wide'), may hold values from -3 to 3
- order_table: int32 [1024], replicated, may hold values from 0 to 1023, each once
- thresholds: float32 [512], replicated, may hold values from 0.2 to 2
Outputs:
- lowrank: float32 [64, 2048, 512], P('wide', 'narrow')
- sparse: float32 [64, 2048, 512], P('wide', 'narrow')
Inputs may be any that keep to these rules, and one draw needn't show every extreme that they name: `order_table`: each order 0 to 1023 stands in exactly one slot.
All inputs are finite; a program needn't handle non-finite values.
Results may differ from a plain program's by a relative error of at most 0.0003.
Values sent between devices are 32-bit elements; how exact they have to be, the bound alone decides.
A program may use at most 128 MiB of HBM per device.

v0:
```python
import math
import jax
import jax.numpy as jnp
from jax import lax
from jax.sharding import PartitionSpec as P

NPIX = 2048
ITERS = 2


def soft_shrink(values, limits):
    return jnp.sign(values) * jnp.maximum(jnp.abs(values) - limits, 0.0)


def wiener_filter(covariance):
    chan_total = covariance.shape[0]
    ridge_shift = jnp.trace(covariance) / chan_total
    factor = jnp.linalg.cholesky(
        covariance + ridge_shift * jnp.eye(chan_total, dtype=covariance.dtype)
    )
    return jax.scipy.linalg.cho_solve((factor, True), covariance)


def per_device(coeffs, legendre, order_table, thresholds):
    slot_count = legendre.shape[0]
    degrees = legendre.shape[2]
    first_slot = lax.axis_index("wide") * slot_count
    own_orders = lax.dynamic_slice_in_dim(order_table, first_slot, slot_count)
    degree_mask = (
        lax.broadcasted_iota(jnp.int32, (slot_count, degrees), 1) >= own_orders[:, None]
    ).astype(legendre.dtype)
    masked = legendre * degree_mask[:, None, :]
    spectra = jnp.einsum("srl,kslc->ksrc", masked, coeffs, preferred_element_type=jnp.float32)
    pixels = lax.broadcasted_iota(jnp.int32, (1, NPIX), 1)
    pixel_phase = order_table[:, None] * pixels % NPIX
    pixel_angle = pixel_phase.astype(jnp.float32) * (2.0 * math.pi / NPIX)
    weights = jnp.where(order_table == 0, 1.0, 2.0).astype(jnp.float32)[:, None]
    cycle_table = jnp.stack([weights * jnp.cos(pixel_angle), -weights * jnp.sin(pixel_angle)])
    sky_map = jnp.einsum(
        "ksrc,ksj->rjc",
        lax.all_to_all(spectra, "wide", split_axis=2, concat_axis=1, tiled=True),
        cycle_table,
        precision=lax.Precision.HIGHEST,
        preferred_element_type=jnp.float32,
    )
    spectra_rows = lax.all_to_all(sky_map, "narrow", split_axis=1, concat_axis=2, tiled=True)
    cycle_count, pixel_count, chan_count = spectra_rows.shape
    sky_field = spectra_rows.reshape(cycle_count * pixel_count, chan_count)
    lowrank = jnp.zeros_like(sky_field)
    sparse = jnp.zeros_like(sky_field)
    for iteration in range(ITERS):
        sparse = soft_shrink(sky_field - lowrank, thresholds)
        residue = sky_field - sparse
        partial_cov = jnp.dot(
            residue.T, residue, precision=lax.Precision.HIGHEST, preferred_element_type=jnp.float32
        )
        covariance = lax.psum(partial_cov, ("wide", "narrow"))
        lowrank = jnp.dot(
            residue,
            wiener_filter(covariance),
            precision=lax.Precision.HIGHEST,
            preferred_element_type=jnp.float32,
        )
    return (
        lowrank.reshape(cycle_count, pixel_count, chan_count),
        sparse.reshape(cycle_count, pixel_count, chan_count),
    )


def solution(mesh):
    placed = (P(None, "wide", None, "narrow"), P("wide", None, None), P(), P())
    return jax.shard_map(
        per_device,
        mesh=mesh,
        in_specs=placed,
        out_specs=(P("wide", "narrow", None), P("wide", "narrow", None)),
        check_vma=False,
    )
```

profile of v0, /device:TPU:2, one launch (start us, length us, event | category | flops | bytes accessed | tf_op | source)
XLA Modules:
  0.0 966.5 jit_solution(3870654779187750146)
XLA Ops:
  15.3 12.0 %all-to-all-start = ((f32[2,16,64,128]{3,0,1,2:T(2,128)}), f32[2,16,64,128]{3,0,1,2:T(2,128)S(1)}, u32[]{:S(2)}, u32[]{:S(2)}) async-start(f32[2,16,64,128]{3,0,1,2:T(2,128)} %copy.24), calls=%async_computation | async-start | bytes 2097152 | tf_op jit(solution)/shard_map/all_to_all | solution.py:41
  27.4 35.0 %cosine_multiply_fusion = (f32[1,1024,2048]{1,2,0:T(8,128)}, f32[1,1024,2048]{1,2,0:T(8,128)}) fusion(s32[1024]{0:T(1024)S(1)} %copy-done.7, f32[1024]{0:T(1024)S(1)} %get-tuple-element.68, f32[1024]{0:T(1024)S(1)} %get-tuple-element.69), kind=kLoop, calls=%fused_computation.17 | loop fusion | flops 33554432 | bytes 16789504 | tf_op jit(solution)/shard_map/mul | solution.py:38
  62.4 16.5 %fusion = f32[2048,128,1]{1,0,2:T(8,128)S(1)} fusion(f32[2,1024,128]{2,1,0:T(8,128)S(1)} %bitcast.179, f32[1,1024,2048]{1,2,0:T(8,128)} %get-tuple-element.67, f32[1,1024,2048]{1,2,0:T(8,128)} %get-tuple-element.66), kind=kOutput, calls=%fused_computation.4 | convolution fusion | flops 6446645248 | bytes 18874368 | tf_op jit(solution)/shard_map/ksrc,ksj->rjc/dot_general | solution.py:39
  79.0 19.9 %all_to_all.30 = f32[1,2048,128]{2,0,1:T(1,128)S(1)} all-to-all(f32[1,2048,128]{2,0,1:T(1,128)S(1)} %bitcast.180), channel_id=1, replica_groups=mesh['wide'=64,'narrow'=4] {'narrow'}, dimensions={1} | all-to-all | bytes 2097152 | tf_op jit(solution)/shard_map/all_to_all | solution.py:46
  104.0 256.8 %all-reduce.4.cloned.1.call-done = f32[512,512]{0,1:T(8,128)} async-done(((f32[512,512]{0,1:T(8,128)}), f32[512,512]{0,1:T(8,128)}) %all-reduce.4.cloned.1.call-update) | async-done | bytes 1048592 | tf_op jit(solution)/shard_map/psum | solution.py:57
  368.8 11.7 %cholesky.286 = f32[128,128]{1,0:T(8,128)S(1)} custom-call(f32[128,128]{1,0:T(8,128)S(1)} %cholesky.426), custom_call_target="Cholesky" | custom-call | tf_op jit(solution)/shard_map/jit(cholesky)/cholesky | solution.py:18
  380.5 9.8 %custom-call.29 = f32[1,128,128]{1,2,0:T(8,128)S(1)} custom-call(f32[1,128,128]{2,1,0:T(8,128)S(1)} %get-tuple-element.65), custom_call_target="InvertDiagBlocksLowerTriangular" | custom-call | tf_op jit(solution)/shard_map/jit(cholesky)/cholesky | solution.py:18
  393.0 11.7 %cholesky.305 = f32[128,128]{1,0:T(8,128)S(1)} custom-call(f32[128,128]{1,0:T(8,128)S(1)} %cholesky.430), custom_call_target="Cholesky" | custom-call | tf_op jit(solution)/shard_map/jit(cholesky)/cholesky | solution.py:18
  404.7 18.5 %custom-call.30 = f32[1,128,128]{1,2,0:T(8,128)S(1)} custom-call(f32[1,128,128]{2,1,0:T(8,128)S(1)} %get-tuple-element.62), custom_call_target="InvertDiagBlocksLowerTriangular" | custom-call | tf_op jit(solution)/shard_map/jit(cholesky)/cholesky | solution.py:18
  424.8 11.7 %cholesky.326 = f32[128,128]{1,0:T(8,128)S(1)} custom-call(f32[128,128]{1,0:T(8,128)S(1)} %cholesky.435), custom_call_target="Cholesky" | custom-call | tf_op jit(solution)/shard_map/jit(cholesky)/cholesky | solution.py:18
  437.2 9.8 %custom-call.31 = f32[1,128,128]{1,2,0:T(8,128)S(1)} custom-call(f32[1,128,128]{2,1,0:T(8,128)S(1)} %get-tuple-element.59), custom_call_target="InvertDiagBlocksLowerTriangular" | custom-call | tf_op jit(solution)/shard_map/jit(cholesky)/cholesky | solution.py:18
  448.5 12.1 %cholesky.343 = f32[128,128]{1,0:T(8,128)S(1)} custom-call(f32[128,128]{1,0:T(8,128)S(1)} %convolution_subtract_fusion.18), custom_call_target="Cholesky" | custom-call | tf_op jit(solution)/shard_map/jit(cholesky)/cholesky | solution.py:18
  465.6 11.2 %while.4 = (s32[]{:T(128)}, f32[512,512]{1,0:T(8,128)}, s32[4,2]{0,1:T(2,128)S(1)}, f32[4,128,128]{2,1,0:T(8,128)S(1)}, s32[]{:T(128)}) while((s32[]{:T(128)}, f32[512,512]{1,0:T(8,128)}, s32[4,2]{0,1:T(2,128)S(1)}, f32[4,128,128]{2,1,0:T(8,128)S(1)}, s32[]{:T(128)}) %tuple.61), condition=%wide.while_cond, body=%wide.while_body.sunk | while | flops 2 | bytes 131181 | solution.py:21
  477.6 40.1 %custom-call.32 = f32[4,128,128]{1,2,0:T(8,128)S(1)} custom-call(f32[4,128,128]{2,1,0:T(8,128)} %copy-done.5), custom_call_target="InvertDiagBlocksLowerTriangular" | custom-call | tf_op jit(solution)/shard_map/jit(_cho_solve)/triangular_solve | solution.py:21
  539.6 255.4 %all-reduce.6.cloned.1.call-done = f32[512,512]{0,1:T(8,128)} async-done(((f32[512,512]{0,1:T(8,128)}), f32[512,512]{0,1:T(8,128)}) %all-reduce.6.cloned.1.call-update) | async-done | bytes 1048592 | tf_op jit(solution)/shard_map/psum | solution.py:57
  803.1 11.9 %cholesky.358 = f32[128,128]{1,0:T(8,128)S(1)} custom-call(f32[128,128]{1,0:T(8,128)S(1)} %cholesky.439), custom_call_target="Cholesky" | custom-call | tf_op jit(solution)/shard_map/jit(cholesky)/cholesky | solution.py:18
  815.1 9.8 %custom-call.33 = f32[1,128,128]{1,2,0:T(8,128)S(1)} custom-call(f32[1,128,128]{2,1,0:T(8,128)S(1)} %get-tuple-element.55), custom_call_target="InvertDiagBlocksLowerTriangular" | custom-call | tf_op jit(solution)/shard_map/jit(cholesky)/cholesky | solution.py:18
  827.5 11.7 %cholesky.377 = f32[128,128]{1,0:T(8,128)S(1)} custom-call(f32[128,128]{1,0:T(8,128)S(1)} %cholesky.443), custom_call_target="Cholesky" | custom-call | tf_op jit(solution)/shard_map/jit(cholesky)/cholesky | solution.py:18
  840.6 10.0 %custom-call.34 = f32[1,128,128]{1,2,0:T(8,128)S(1)} custom-call(f32[1,128,128]{2,1,0:T(8,128)S(1)} %get-tuple-element.52), custom_call_target="InvertDiagBlocksLowerTriangular" | custom-call | tf_op jit(solution)/shard_map/jit(cholesky)/cholesky | solution.py:18
  852.1 11.7 %cholesky.398 = f32[128,128]{1,0:T(8,128)S(1)} custom-call(f32[128,128]{1,0:T(8,128)S(1)} %cholesky.448), custom_call_target="Cholesky" | custom-call | tf_op jit(solution)/shard_map/jit(cholesky)/cholesky | solution.py:18
  864.5 9.8 %custom-call.35 = f32[1,128,128]{1,2,0:T(8,128)S(1)} custom-call(f32[1,128,128]{2,1,0:T(8,128)S(1)} %get-tuple-element.49), custom_call_target="InvertDiagBlocksLowerTriangular" | custom-call | tf_op jit(solution)/shard_map/jit(cholesky)/cholesky | solution.py:18
  875.8 11.7 %cholesky.415 = f32[128,128]{1,0:T(8,128)S(1)} custom-call(f32[128,128]{1,0:T(8,128)S(1)} %convolution_subtract_fusion.17), custom_call_target="Cholesky" | custom-call | tf_op jit(solution)/shard_map/jit(cholesky)/cholesky | solution.py:18
  891.8 11.7 %while.5 = (s32[]{:T(128)}, f32[512,512]{1,0:T(8,128)}, s32[4,2]{0,1:T(2,128)S(1)}, f32[4,128,128]{2,1,0:T(8,128)S(1)}, s32[]{:T(128)}) while((s32[]{:T(128)}, f32[512,512]{1,0:T(8,128)}, s32[4,2]{0,1:T(2,128)S(1)}, f32[4,128,128]{2,1,0:T(8,128)S(1)}, s32[]{:T(128)}) %tuple.71), condition=%wide.while_cond.clone, body=%wide.while_body.clone.sunk | while | flops 2 | bytes 131181 | solution.py:21
  903.6 39.6 %custom-call.36 = f32[4,128,128]{1,2,0:T(8,128)S(1)} custom-call(f32[4,128,128]{2,1,0:T(8,128)S(1)} %get-tuple-element.19), custom_call_target="InvertDiagBlocksLowerTriangular" | custom-call | tf_op jit(solution)/shard_map/jit(_cho_solve)/triangular_solve | solution.py:21
  (136 shorter events, 107.6 us)
Async XLA Ops:
  8.0 19.3 %copy-start.7 = (s32[1024]{0:T(1024)S(1)}, s32[1024]{0:T(1024)}, u32[]{:S(2)}) copy-start(s32[1024]{0:T(1024)} %param.9) | copy-start | bytes 12292
  15.3 47.1 %all-to-all-start = ((f32[2,16,64,128]{3,0,1,2:T(2,128)}), f32[2,16,64,128]{3,0,1,2:T(2,128)S(1)}, u32[]{:S(2)}, u32[]{:S(2)}) async-start(f32[2,16,64,128]{3,0,1,2:T(2,128)} %copy.24), calls=%async_computation | async-start | bytes 2097152 | tf_op jit(solution)/shard_map/all_to_all | solution.py:41
  27.3 333.4 %all-reduce.4.cloned.1.call-start = ((), (), s32[]{:S(2)}) async-start(), calls=%async_computation.2 | async-start | bytes 2097152 | tf_op jit(solution)/shard_map/psum | solution.py:57
  62.4 36.8 %copy-start.6 = (f32[512]{0:T(512)S(1)}, f32[512]{0:T(512)}, u32[]{:S(2)}) copy-start(f32[512]{0:T(512)} %param.10) | copy-start | bytes 6148
  102.5 692.5 %all-reduce.6.cloned.1.call-start = ((), (), s32[]{:S(2)}) async-start(), calls=%async_computation.3 | async-start | bytes 2097152 | tf_op jit(solution)/shard_map/psum | solution.py:57
  360.7 157.0 %copy-start = (f32[512,512]{0,1:T(8,128)S(1)}, f32[512,512]{0,1:T(8,128)}, u32[]{:S(2)}) copy-start(f32[512,512]{0,1:T(8,128)} %all-reduce.4.cloned.1.call-done) | copy-start | bytes 3145732
  367.8 1.0 copy-start.4
  465.6 65.4 %copy-start.2 = (f32[512,512]{0,1:T(8,128)S(1)}, f32[512,512]{0,1:T(8,128)}, u32[]{:S(2)}) copy-start(f32[512,512]{0,1:T(8,128)} %bitcast_subtract_fusion.1) | copy-start | bytes 3145732
  476.8 0.7 copy-start.5
  795.1 148.1 %copy-start.1 = (f32[512,512]{0,1:T(8,128)S(1)}, f32[512,512]{0,1:T(8,128)}, u32[]{:S(2)}) copy-start(f32[512,512]{0,1:T(8,128)} %all-reduce.6.cloned.1.call-done) | copy-start | bytes 3145732
  802.1 1.0 copy-start.3
Sparse Core Ops, SparseCore 0:
  102.6 258.0 all-reduce.3
  537.2 257.7 all-reduce.5
where the time goes:
time: 975 us; the launch traced here: 966 us
  waiting for transfers between devices  512 us (53%)
  other arithmetic  296 us (30%)
  matrix products  71 us (7%)
  local copies, waits for them, and re-layouts  33.9 us (3%)
  between operations  21.4 us (2%)
  blocking collectives  19.9 us (2%)
  starting transfers between devices  12.1 us (1%)
    psum x2, waiting for transfers between devices, per_device(): covariance = lax.psum(partial_cov, ('wide', 'narrow'))  512 us
    another operation x29, other arithmetic, wiener_filter(): jnp.linalg.cholesky(covariance + ridge_shift * jnp.eye(chan_total, dtype=...  167 us
    another operation x5, other arithmetic, wiener_filter(): return jax.scipy.linalg.cho_solve((factor, True), covariance)  81.9 us
    mul x1, other arithmetic, per_device(): weights * jnp.cos(pixel_angle)  35 us
    another operation x28, matrix products, wiener_filter(): return jax.scipy.linalg.cho_solve((factor, True), covariance)  26.2 us
    another operation x27, local copies, waits for them, and re-layouts, wiener_filter(): return jax.scipy.linalg.cho_solve((factor, True), covariance)  22.8 us
    all_to_all x1, blocking collectives, per_device(): lax.all_to_all(sky_map, 'narrow', split_axis=1, concat_axis=2, tiled=True)  19.9 us
  transfers between devices with their start and end apart: 3, of which 2 were waited for; matrix products, arithmetic and copies ran while one was open for 4% of the time, Pallas kernels for 0%

commit v1 on v0

--- a/solution.py
+++ b/solution.py
@@ -54,7 +54,9 @@
         partial_cov = jnp.dot(
             residue.T, residue, precision=lax.Precision.HIGHEST, preferred_element_type=jnp.float32
         )
-        covariance = lax.psum(partial_cov, ("wide", "narrow"))
+        covariance = partial_cov
+        for name in ("wide", "narrow"):
+            covariance = lax.psum(covariance, name)
         lowrank = jnp.dot(
             residue,
             wiener_filter(covariance),

time: 975 us -> 935 us (0.959)
  waiting for transfers between devices: 512 us -> 472 us
    psum x2 -> x4, waiting for transfers between devices: 512 us -> 472 us  [per_device(): covariance = lax.psum(covariance, name)]
  transfers between devices with their start and end apart: 3 -> 5, of which waited for: 2 -> 4; matrix products, arithmetic and copies ran while one was open for 4% -> 4% of each run, Pallas kernels for 0% -> 0%
where the time goes in v1:
time: 935 us; the launch traced here: 926 us
  waiting for transfers between devices  472 us (50%)
  other arithmetic  296 us (32%)
  matrix products  70.9 us (8%)
  local copies, waits for them, and re-layouts  34.3 us (4%)
  between operations  21.2 us (2%)
  blocking collectives  19.9 us (2%)
  starting transfers between devices  12.3 us (1%)
    psum x4, waiting for transfers between devices, per_device(): covariance = lax.psum(covariance, name)  472 us
    another operation x29, other arithmetic, wiener_filter(): jnp.linalg.cholesky(covariance + ridge_shift * jnp.eye(chan_total, dtype=...  167 us
    another operation x5, other arithmetic, wiener_filter(): return jax.scipy.linalg.cho_solve((factor, True), covariance)  81.6 us
    mul x1, other arithmetic, per_device(): weights * jnp.cos(pixel_angle)  35 us
    another operation x28, matrix products, wiener_filter(): return jax.scipy.linalg.cho_solve((factor, True), covariance)  26.2 us
    another operation x27, local copies, waits for them, and re-layouts, wiener_filter(): return jax.scipy.linalg.cho_solve((factor, True), covariance)  23.3 us
    all_to_all x1, blocking collectives, per_device(): lax.all_to_all(sky_map, 'narrow', split_axis=1, concat_axis=2, tiled=True)  19.9 us
  transfers between devices with their start and end apart: 5, of which 4 were waited for; matrix products, arithmetic and copies ran while one was open for 4% of the time, Pallas kernels for 0%

profile of v1, /device:TPU:2, one launch (start us, length us, event | category | flops | bytes accessed | tf_op | source)
XLA Modules:
  0.0 926.3 jit_solution(7749570123790843614)
XLA Ops:
  15.3 12.0 %all-to-all-start = ((f32[2,16,64,128]{3,0,1,2:T(2,128)}), f32[2,16,64,128]{3,0,1,2:T(2,128)S(1)}, u32[]{:S(2)}, u32[]{:S(2)}) async-start(f32[2,16,64,128]{3,0,1,2:T(2,128)} %copy.24), calls=%async_computation | async-start | bytes 2097152 | tf_op jit(solution)/shard_map/all_to_all | solution.py:41
  27.4 35.0 %cosine_multiply_fusion = (f32[1,1024,2048]{1,2,0:T(8,128)}, f32[1,1024,2048]{1,2,0:T(8,128)}) fusion(s32[1024]{0:T(1024)S(1)} %copy-done.7, f32[1024]{0:T(1024)S(1)} %get-tuple-element.68, f32[1024]{0:T(1024)S(1)} %get-tuple-element.69), kind=kLoop, calls=%fused_computation.17 | loop fusion | flops 33554432 | bytes 16789504 | tf_op jit(solution)/shard_map/mul | solution.py:38
  62.4 16.5 %fusion = f32[2048,128,1]{1,0,2:T(8,128)S(1)} fusion(f32[2,1024,128]{2,1,0:T(8,128)S(1)} %bitcast.179, f32[1,1024,2048]{1,2,0:T(8,128)} %get-tuple-element.67, f32[1,1024,2048]{1,2,0:T(8,128)} %get-tuple-element.66), kind=kOutput, calls=%fused_computation.4 | convolution fusion | flops 6446645248 | bytes 18874368 | tf_op jit(solution)/shard_map/ksrc,ksj->rjc/dot_general | solution.py:39
  79.0 19.9 %all_to_all.30 = f32[1,2048,128]{2,0,1:T(1,128)S(1)} all-to-all(f32[1,2048,128]{2,0,1:T(1,128)S(1)} %bitcast.180), channel_id=1, replica_groups=mesh['wide'=64,'narrow'=4] {'narrow'}, dimensions={1} | all-to-all | bytes 2097152 | tf_op jit(solution)/shard_map/all_to_all | solution.py:46
  102.6 186.3 %all-reduce.6.cloned.1.call-done = f32[512,512]{0,1:T(8,128)} async-done(((f32[512,512]{0,1:T(8,128)}), f32[512,512]{0,1:T(8,128)}) %all-reduce.6.cloned.1.call-update) | async-done | bytes 1048592 | tf_op jit(solution)/shard_map/psum | solution.py:59
  290.3 49.4 %all-reduce.8.cloned.1.call-done = f32[512,512]{0,1:T(8,128)} async-done(((f32[512,512]{0,1:T(8,128)}), f32[512,512]{0,1:T(8,128)}) %all-reduce.8.cloned.1.call-update) | async-done | bytes 1048592 | tf_op jit(solution)/shard_map/psum | solution.py:59
  347.7 11.7 %cholesky.286 = f32[128,128]{1,0:T(8,128)S(1)} custom-call(f32[128,128]{1,0:T(8,128)S(1)} %cholesky.426), custom_call_target="Cholesky" | custom-call | tf_op jit(solution)/shard_map/jit(cholesky)/cholesky | solution.py:18
  359.5 9.8 %custom-call.29 = f32[1,128,128]{1,2,0:T(8,128)S(1)} custom-call(f32[1,128,128]{2,1,0:T(8,128)S(1)} %get-tuple-element.65), custom_call_target="InvertDiagBlocksLowerTriangular" | custom-call | tf_op jit(solution)/shard_map/jit(cholesky)/cholesky | solution.py:18
  371.9 11.7 %cholesky.305 = f32[128,128]{1,0:T(8,128)S(1)} custom-call(f32[128,128]{1,0:T(8,128)S(1)} %cholesky.430), custom_call_target="Cholesky" | custom-call | tf_op jit(solution)/shard_map/jit(cholesky)/cholesky | solution.py:18
  383.7 18.5 %custom-call.30 = f32[1,128,128]{1,2,0:T(8,128)S(1)} custom-call(f32[1,128,128]{2,1,0:T(8,128)S(1)} %get-tuple-element.62), custom_call_target="InvertDiagBlocksLowerTriangular" | custom-call | tf_op jit(solution)/shard_map/jit(cholesky)/cholesky | solution.py:18
  403.8 11.7 %cholesky.326 = f32[128,128]{1,0:T(8,128)S(1)} custom-call(f32[128,128]{1,0:T(8,128)S(1)} %cholesky.435), custom_call_target="Cholesky" | custom-call | tf_op jit(solution)/shard_map/jit(cholesky)/cholesky | solution.py:18
  427.5 12.1 %cholesky.343 = f32[128,128]{1,0:T(8,128)S(1)} custom-call(f32[128,128]{1,0:T(8,128)S(1)} %convolution_subtract_fusion.18), custom_call_target="Cholesky" | custom-call | tf_op jit(solution)/shard_map/jit(cholesky)/cholesky | solution.py:18
  444.6 11.7 %while.4 = (s32[]{:T(128)}, f32[512,512]{1,0:T(8,128)}, s32[4,2]{0,1:T(2,128)S(1)}, f32[4,128,128]{2,1,0:T(8,128)S(1)}, s32[]{:T(128)}) while((s32[]{:T(128)}, f32[512,512]{1,0:T(8,128)}, s32[4,2]{0,1:T(2,128)S(1)}, f32[4,128,128]{2,1,0:T(8,128)S(1)}, s32[]{:T(128)}) %tuple.61), condition=%wide.while_cond, body=%wide.while_body.sunk | while | flops 2 | bytes 131181 | solution.py:21
  457.0 40.1 %custom-call.32 = f32[4,128,128]{1,2,0:T(8,128)S(1)} custom-call(f32[4,128,128]{2,1,0:T(8,128)} %copy-done.5), custom_call_target="InvertDiagBlocksLowerTriangular" | custom-call | tf_op jit(solution)/shard_map/jit(_cho_solve)/triangular_solve | solution.py:21
  516.7 187.9 %all-reduce.10.cloned.1.call-done = f32[512,512]{0,1:T(8,128)} async-done(((f32[512,512]{0,1:T(8,128)}), f32[512,512]{0,1:T(8,128)}) %all-reduce.10.cloned.1.call-update) | async-done | bytes 1048592 | tf_op jit(solution)/shard_map/psum | solution.py:59
  707.2 48.1 %all-reduce.12.cloned.1.call-done = f32[512,512]{0,1:T(8,128)} async-done(((f32[512,512]{0,1:T(8,128)}), f32[512,512]{0,1:T(8,128)}) %all-reduce.12.cloned.1.call-update) | async-done | bytes 1048592 | tf_op jit(solution)/shard_map/psum | solution.py:59
  763.4 11.7 %cholesky.358 = f32[128,128]{1,0:T(8,128)S(1)} custom-call(f32[128,128]{1,0:T(8,128)S(1)} %cholesky.439), custom_call_target="Cholesky" | custom-call | tf_op jit(solution)/shard_map/jit(cholesky)/cholesky | solution.py:18
  775.3 9.8 %custom-call.33 = f32[1,128,128]{1,2,0:T(8,128)S(1)} custom-call(f32[1,128,128]{2,1,0:T(8,128)S(1)} %get-tuple-element.55), custom_call_target="InvertDiagBlocksLowerTriangular" | custom-call | tf_op jit(solution)/shard_map/jit(cholesky)/cholesky | solution.py:18
  787.6 11.7 %cholesky.377 = f32[128,128]{1,0:T(8,128)S(1)} custom-call(f32[128,128]{1,0:T(8,128)S(1)} %cholesky.443), custom_call_target="Cholesky" | custom-call | tf_op jit(solution)/shard_map/jit(cholesky)/cholesky | solution.py:18
  800.7 10.0 %custom-call.34 = f32[1,128,128]{1,2,0:T(8,128)S(1)} custom-call(f32[1,128,128]{2,1,0:T(8,128)S(1)} %get-tuple-element.52), custom_call_target="InvertDiagBlocksLowerTriangular" | custom-call | tf_op jit(solution)/shard_map/jit(cholesky)/cholesky | solution.py:18
  812.3 11.7 %cholesky.398 = f32[128,128]{1,0:T(8,128)S(1)} custom-call(f32[128,128]{1,0:T(8,128)S(1)} %cholesky.448), custom_call_target="Cholesky" | custom-call | tf_op jit(solution)/shard_map/jit(cholesky)/cholesky | solution.py:18
  835.9 11.9 %cholesky.415 = f32[128,128]{1,0:T(8,128)S(1)} custom-call(f32[128,128]{1,0:T(8,128)S(1)} %convolution_subtract_fusion.17), custom_call_target="Cholesky" | custom-call | tf_op jit(solution)/shard_map/jit(cholesky)/cholesky | solution.py:18
  852.2 11.7 %while.5 = (s32[]{:T(128)}, f32[512,512]{1,0:T(8,128)}, s32[4,2]{0,1:T(2,128)S(1)}, f32[4,128,128]{2,1,0:T(8,128)S(1)}, s32[]{:T(128)}) while((s32[]{:T(128)}, f32[512,512]{1,0:T(8,128)}, s32[4,2]{0,1:T(2,128)S(1)}, f32[4,128,128]{2,1,0:T(8,128)S(1)}, s32[]{:T(128)}) %tuple.75), condition=%wide.while_cond.clone, body=%wide.while_body.clone.sunk | while | flops 2 | bytes 131181 | solution.py:21
  863.9 39.3 %custom-call.36 = f32[4,128,128]{1,2,0:T(8,128)S(1)} custom-call(f32[4,128,128]{2,1,0:T(8,128)S(1)} %get-tuple-element.19), custom_call_target="InvertDiagBlocksLowerTriangular" | custom-call | tf_op jit(solution)/shard_map/jit(_cho_solve)/triangular_solve | solution.py:21
  (142 shorter events, 127.9 us)
Async XLA Ops:
  8.0 19.3 %copy-start.7 = (s32[1024]{0:T(1024)S(1)}, s32[1024]{0:T(1024)}, u32[]{:S(2)}) copy-start(s32[1024]{0:T(1024)} %param.9) | copy-start | bytes 12292
  15.3 47.1 %all-to-all-start = ((f32[2,16,64,128]{3,0,1,2:T(2,128)}), f32[2,16,64,128]{3,0,1,2:T(2,128)S(1)}, u32[]{:S(2)}, u32[]{:S(2)}) async-start(f32[2,16,64,128]{3,0,1,2:T(2,128)} %copy.24), calls=%async_computation | async-start | bytes 2097152 | tf_op jit(solution)/shard_map/all_to_all | solution.py:41
  27.3 261.6 %all-reduce.6.cloned.1.call-start = ((), (), s32[]{:S(2)}) async-start(), calls=%async_computation.2 | async-start | bytes 2097152 | tf_op jit(solution)/shard_map/psum | solution.py:59
  62.4 36.8 %copy-start.6 = (f32[512]{0:T(512)S(1)}, f32[512]{0:T(512)}, u32[]{:S(2)}) copy-start(f32[512]{0:T(512)} %param.10) | copy-start | bytes 6148
  102.5 237.2 %all-reduce.8.cloned.1.call-start = ((), (), s32[]{:S(2)}) async-start(), calls=%async_computation.3 | async-start | bytes 2097152 | tf_op jit(solution)/shard_map/psum | solution.py:59
  288.9 415.8 %all-reduce.10.cloned.1.call-start = ((), (), s32[]{:S(2)}) async-start(), calls=%async_computation.4 | async-start | bytes 2097152 | tf_op jit(solution)/shard_map/psum | solution.py:59
  339.7 157.5 %copy-start = (f32[512,512]{0,1:T(8,128)S(1)}, f32[512,512]{0,1:T(8,128)}, u32[]{:S(2)}) copy-start(f32[512,512]{0,1:T(8,128)} %all-reduce.8.cloned.1.call-done) | copy-start | bytes 3145732
  346.7 1.0 copy-start.4
  444.6 65.8 %copy-start.2 = (f32[512,512]{0,1:T(8,128)S(1)}, f32[512,512]{0,1:T(8,128)}, u32[]{:S(2)}) copy-start(f32[512,512]{0,1:T(8,128)} %bitcast_subtract_fusion.1) | copy-start | bytes 3145732
  456.3 0.7 copy-start.5
  516.5 238.8 %all-reduce.12.cloned.1.call-start = ((), (), s32[]{:S(2)}) async-start(), calls=%async_computation.5 | async-start | bytes 2097152 | tf_op jit(solution)/shard_map/psum | solution.py:59
  755.3 147.9 %copy-start.1 = (f32[512,512]{0,1:T(8,128)S(1)}, f32[512,512]{0,1:T(8,128)}, u32[]{:S(2)}) copy-start(f32[512,512]{0,1:T(8,128)} %all-reduce.12.cloned.1.call-done) | copy-start | bytes 3145732
  762.4 1.0 copy-start.3
Sparse Core Ops, SparseCore 0:
  102.6 186.1 all-reduce.5
  291.2 48.4 all-reduce.7
  516.6 187.9 all-reduce.9
  706.9 48.4 all-reduce.11
